TPU v7x, 32 devices: a whole 2x2x4 slice. The times are simulated.
32 devices in a mesh: grp: 4 (over z), ctx: 8 (over y, x, core).
Axes of the slice: x: 2, y: 2, z: 4, core: 2. Of those that a mesh axis runs over, the one named last changes fastest.
Arguments:
- query_rows: bfloat16 [32768, 512], P(('grp', 'ctx')), may hold values from -6 to 6
- key_rows: bfloat16 [32768, 512], P(('grp', 'ctx')), may hold values from -6 to 6
- value_rows: bfloat16 [32768, 512], P(('grp', 'ctx')), may hold values from -6 to 6
- cluster_ids: int32 [4, 32768], P(None, ('grp', 'ctx')), may hold values from 0 to 255, as said below
Outputs:
- attended: bfloat16 [32768, 512], P(('grp', 'ctx'))
Inputs may be any that keep to these rules, and one draw needn't show every extreme that they name: `cluster_ids`: for each head, the tokens of one device whose clusters share one value of id // 8 number at most 96; for each head one such range receives exactly 96 tokens from every device, and every other range at most 32 from one device. For each head and range, the sum over its clusters of their token counts rounded up to multiples of 128 is at most 3072, with equality for the range that is full.
All inputs are finite; a program needn't handle non-finite values.
Results may differ from a plain program's by a relative error of at most 0.0034.
Values may be sent and summed in bfloat16 or wider, within the bound.
A program may use at most 128 MiB of HBM per device.

v0:
```python
import math

import jax
import jax.numpy as jnp
from jax import lax
from jax.sharding import PartitionSpec as P

CL_DEV = 8
TILE = 128
WORK = 3072


NEG_FILL = -1e30


def cluster_attention(packed_rows, labels, used_rows):
    head_width = packed_rows.shape[1] // 3
    total_rows = packed_rows.shape[0]
    block_rows = math.gcd(total_rows, 512)
    score_scale = head_width ** (-0.5)
    queries = packed_rows[:, :head_width]
    keys_all = packed_rows[:, head_width : 2 * head_width]
    values_all = packed_rows[:, 2 * head_width :]
    positions = jnp.arange(total_rows, dtype=jnp.int32)
    previous = jnp.concatenate([jnp.full((1,), -2, jnp.int32), labels[:-1]])
    starts_here = (labels != previous) & (labels >= 0)
    region_start = lax.cummax(jnp.where(starts_here, positions, 0), axis=0)
    first_live = jnp.min(
        jnp.where(labels >= 0, region_start, total_rows).reshape(-1, block_rows), axis=1
    )
    block_count = (used_rows + block_rows - 1) // block_rows

    def query_block(block_index, result):
        row_start = block_index * block_rows
        query_part = lax.dynamic_slice_in_dim(queries, row_start, block_rows, 0)
        query_label = lax.dynamic_slice_in_dim(labels, row_start, block_rows, 0)
        query_pos = row_start + jnp.arange(block_rows, dtype=jnp.int32)

        def key_block(key_index, state_now):
            run_max, run_sum, weighted = state_now
            key_start = key_index * block_rows
            key_part = lax.dynamic_slice_in_dim(keys_all, key_start, block_rows, 0)
            value_part = lax.dynamic_slice_in_dim(values_all, key_start, block_rows, 0)
            key_label = lax.dynamic_slice_in_dim(labels, key_start, block_rows, 0)
            key_pos = key_start + jnp.arange(block_rows, dtype=jnp.int32)
            scores = (
                jnp.dot(query_part, key_part.T, preferred_element_type=jnp.float32) * score_scale
            )
            allowed = (
                (query_label[:, None] == key_label[None, :])
                & (key_pos[None, :] <= query_pos[:, None])
                & (query_label[:, None] >= 0)
            )
            masked = jnp.where(allowed, scores, NEG_FILL)
            new_max = jnp.maximum(run_max, jnp.max(masked, axis=1))
            weights = jnp.where(allowed, jnp.exp(masked - new_max[:, None]), 0.0)
            factor = jnp.exp(run_max - new_max)
            run_sum = run_sum * factor + jnp.sum(weights, axis=1)
            weighted = weighted * factor[:, None] + jnp.dot(
                weights.astype(jnp.bfloat16), value_part, preferred_element_type=jnp.float32
            )
            return (new_max, run_sum, weighted)

        start_state = (
            jnp.full((block_rows,), NEG_FILL, jnp.float32),
            jnp.zeros((block_rows,), jnp.float32),
            jnp.zeros((block_rows, head_width), jnp.float32),
        )
        first_block = jnp.minimum(first_live[block_index], row_start) // block_rows
        run_max, run_sum, weighted = lax.fori_loop(
            first_block, block_index + 1, key_block, start_state
        )
        output = (weighted / jnp.where(run_sum > 0.0, run_sum, 1.0)[:, None]).astype(jnp.bfloat16)
        return lax.dynamic_update_slice_in_dim(result, output, row_start, 0)

    return lax.fori_loop(
        0, block_count, query_block, jnp.zeros((total_rows, head_width), jnp.bfloat16)
    )


def serve_items(payload, labels_in):
    lead_shape = labels_in.shape[:-2]
    item_count = labels_in.shape[-2]
    capacity = labels_in.shape[-1]
    source_count = math.prod(lead_shape)
    local_ids = jnp.where(labels_in >= 0, labels_in % CL_DEV, -1)
    member = (local_ids[..., None] == jnp.arange(CL_DEV, dtype=jnp.int32)).astype(jnp.int32)
    per_source = jnp.sum(member, axis=2)
    totals = jnp.sum(per_source, axis=0)
    padded = (totals + TILE - 1) // TILE * TILE
    region = jnp.cumsum(padded, axis=1) - padded
    earlier_sources = jnp.cumsum(per_source, axis=0) - per_source
    within = jnp.cumsum(member, axis=2) - member
    offset = region[None, :, None, :] + earlier_sources[:, :, None, :] + within
    target = jnp.where(local_ids >= 0, jnp.sum(offset * member, axis=3), WORK)
    row_total = source_count * capacity
    replies = []
    for item_pos in range(item_count):
        target_rows = target[:, item_pos].reshape(-1)
        row_data = payload[:, item_pos].reshape(-1, payload.shape[-1])
        label_data = labels_in[:, item_pos].reshape(-1)
        source_of_row = (
            jnp.full((WORK,), row_total, jnp.int32)
            .at[target_rows]
            .set(jnp.arange(row_total, dtype=jnp.int32), mode="drop")
        )
        work_rows = jnp.take(row_data, source_of_row, axis=0, mode="fill", fill_value=0)
        work_labels = jnp.take(label_data, source_of_row, axis=0, mode="fill", fill_value=-1)
        used_rows = jnp.max(jnp.where(target_rows < WORK, target_rows + 1, 0))
        attended = cluster_attention(work_rows, work_labels, used_rows)
        answer_rows = jnp.take(attended, target_rows, axis=0, mode="fill", fill_value=0)
        replies.append(answer_rows.reshape(source_count, capacity, -1))
    answer = jnp.stack(replies, axis=1)
    return answer


def local(query_rows, key_rows, value_rows, cluster_ids):
    groups = lax.axis_size("grp")
    members = lax.axis_size("ctx")
    devices = groups * members
    head_count, tokens = cluster_ids.shape
    head_width = query_rows.shape[1] // head_count
    capacity = 3 * tokens // devices
    owners = cluster_ids // CL_DEV
    onehot = (owners[:, :, None] == jnp.arange(devices, dtype=jnp.int32)).astype(jnp.int32)
    slot_ids = jnp.sum((jnp.cumsum(onehot, axis=1) - onehot) * onehot, axis=2)
    packed = jnp.concatenate(
        [
            query_rows.reshape(tokens, head_count, head_width),
            key_rows.reshape(tokens, head_count, head_width),
            value_rows.reshape(tokens, head_count, head_width),
        ],
        axis=2,
    )
    packed_flat = packed.reshape(tokens * head_count, 3 * head_width)
    head_rows = jnp.broadcast_to(
        jnp.arange(head_count, dtype=jnp.int32)[None, :], (tokens, head_count)
    )
    flat_slot = ((owners.T * head_count + head_rows) * capacity + slot_ids.T).reshape(-1)
    slot_total = devices * head_count * capacity
    source_of_slot = (
        jnp.full((slot_total,), tokens * head_count, jnp.int32)
        .at[flat_slot]
        .set(jnp.arange(tokens * head_count, dtype=jnp.int32))
    )
    outgoing = jnp.take(packed_flat, source_of_slot, axis=0, mode="fill", fill_value=0).reshape(
        devices, head_count, capacity, 3 * head_width
    )
    tagged = jnp.take(
        cluster_ids.T.reshape(-1), source_of_slot, axis=0, mode="fill", fill_value=-1
    ).reshape(devices, head_count, capacity)
    answer = serve_items(
        lax.all_to_all(outgoing, ("grp", "ctx"), split_axis=0, concat_axis=0, tiled=True),
        lax.all_to_all(tagged, ("grp", "ctx"), split_axis=0, concat_axis=0, tiled=True),
    )
    back = lax.all_to_all(answer, ("grp", "ctx"), split_axis=0, concat_axis=0, tiled=True)
    back_flat = back.reshape(slot_total, head_width)
    result = jnp.take(back_flat, flat_slot, axis=0)
    return result.reshape(tokens, head_count * head_width)


def solution(mesh):
    return jax.shard_map(
        local,
        mesh=mesh,
        in_specs=(
            P(("grp", "ctx"), None),
            P(("grp", "ctx"), None),
            P(("grp", "ctx"), None),
            P(None, ("grp", "ctx")),
        ),
        out_specs=P(("grp", "ctx"), None),
        check_vma=False,
    )
```

profile of v0, /device:TPU:0, one launch (start us, length us, event | category | flops | bytes accessed | tf_op | source)
XLA Modules:
  0.0 786.8 jit_solution(8437429449442012175)
XLA Ops:
  1.5 36.0 %reduce-window.40 = s32[4,32,8,128]{3,2,1,0:T(8,128)S(1)} reduce-window(s32[4,32,8,128]{3,2,1,0:T(8,128)S(1)} %fusion.69, s32[]{:T(128)} %constant.503.clone.1), window={size=1x1x1x128 pad=0_0x0_0x0_0x127_0}, to_apply=%region_0.1 | reduce-window | flops 16646144 | bytes 1048580 | tf_op jit(solution)/shard_map/reduce-window
  39.8 15.5 %scatter_custom_fusion = s32[12288]{0:T(1024)S(1)} fusion(s32[4096]{0:T(1024)S(1)} %bitcast.141, s32[4096]{0:T(1024)S(1)} %iota.84, s32[]{:T(128)} %constant.512.clone.1), kind=kCustom, calls=%fused_computation.188 | custom fusion | bytes 49156 | tf_op jit(solution)/shard_map/scatter | solution.py:144
  56.0 68.0 %gather_fusion = s32[12288]{0:T(1024)S(1)} fusion(s32[4096]{0:T(1024)S(1)} %reshape.395, s32[12288]{0:T(1024)S(1)} %fusion.77), kind=kCustom, calls=%fused_computation.12 | custom fusion | bytes 147456 | tf_op jit(solution)/shard_map/jit(_take)/gather | solution.py:149
  125.4 7.3 all-to-all-start
  139.3 49.2 %gather_fusion.1 = bf16[12288,384]{1,0:T(8,128)(2,1)} fusion(bf16[4096,384]{1,0:T(8,128)(2,1)S(1)} %pad_maximum_fusion, s32[12288]{0:T(1024)S(1)} %fusion.77), kind=kCustom, calls=%fused_computation.13 | custom fusion | bytes 18923520 | tf_op jit(solution)/shard_map/jit(_take)/gather | solution.py:146
  188.5 9.4 %broadcast_select_fusion = bf16[32,4,96,384]{3,2,1,0:T(8,128)(2,1)} fusion(bf16[32,4,96,384]{3,2,1,0:T(8,128)(2,1)} %bitcast.132, pred[32,4,96]{2,1,0:T(4,128)(4,1)S(1)} %reduce_and.9), kind=kLoop, calls=%fused_computation.125 | loop fusion | flops 4718592 | bytes 18886656 | tf_op jit(solution)/shard_map/jit(_take)/select_n | solution.py:146
  207.0 10.7 %fusion.64 = s32[32,4,96]{0,1,2:T(4,128)S(1)} fusion(s32[32,4,8]{2,0,1:T(8,128)S(1)} %copy.84, s32[32,4,96]{0,1,2:T(4,128)S(1)} %fusion.71), kind=kOutput, calls=%fused_computation.128 | output fusion | flops 10113024 | bytes 102400 | tf_op jit(solution)/shard_map/jit(cumsum)/reduce_window_sum | solution.py:93
  223.1 11.8 %scatter_custom_fusion.2 = s32[3072]{0:T(1024)S(1)} fusion(s32[3072]{0:T(1024)S(1)} %bitcast.143, s32[3072]{0:T(1024)S(1)} %iota.87, s32[]{:T(128)} %constant.517.clone.1), kind=kCustom, calls=%fused_computation.247 | custom fusion | bytes 12292 | tf_op jit(solution)/shard_map/scatter | solution.py:105
  234.9 17.4 %gather_fusion.6 = s32[3072]{0:T(1024)S(1)} fusion(s32[3072]{0:T(1024)S(1)} %reshape_squeeze.48, s32[3072]{0:T(1024)S(1)} %fusion.93), kind=kCustom, calls=%fused_computation.6.clone | custom fusion | bytes 36864 | tf_op jit(solution)/shard_map/jit(_take)/gather | solution.py:108
  252.3 11.8 %scatter_custom_fusion.1 = s32[3072]{0:T(1024)S(1)} fusion(s32[3072]{0:T(1024)S(1)} %bitcast.144, s32[3072]{0:T(1024)S(1)} %iota.85, s32[]{:T(128)} %constant.517.clone.1), kind=kCustom, calls=%fused_computation.249 | custom fusion | bytes 12292 | tf_op jit(solution)/shard_map/scatter | solution.py:105
  264.2 17.4 %gather_fusion.3 = s32[3072]{0:T(1024)S(1)} fusion(s32[3072]{0:T(1024)S(1)} %reshape_squeeze.44, s32[3072]{0:T(1024)S(1)} %fusion.91), kind=kCustom, calls=%fused_computation.1.clone | custom fusion | bytes 36864 | tf_op jit(solution)/shard_map/jit(_take)/gather | solution.py:108
  287.8 11.8 %scatter_custom_fusion.3 = s32[3072]{0:T(1024)S(1)} fusion(s32[3072]{0:T(1024)S(1)} %bitcast.145, s32[3072]{0:T(1024)S(1)} %iota.89, s32[]{:T(128)} %constant.517.clone.1), kind=kCustom, calls=%fused_computation.245 | custom fusion | bytes 12292 | tf_op jit(solution)/shard_map/scatter | solution.py:105
  299.6 17.4 %gather_fusion.9 = s32[3072]{0:T(1024)S(1)} fusion(s32[3072]{0:T(1024)S(1)} %reshape_squeeze.52, s32[3072]{0:T(1024)S(1)} %fusion.95), kind=kCustom, calls=%fused_computation.7.clone | custom fusion | bytes 36864 | tf_op jit(solution)/shard_map/jit(_take)/gather | solution.py:108
  317.1 12.0 %scatter_custom_fusion.4 = s32[3072]{0:T(1024)S(1)} fusion(s32[3072]{0:T(1024)S(1)} %bitcast.146, s32[3072]{0:T(1024)S(1)} %iota.91, s32[]{:T(128)} %constant.517.clone.1), kind=kCustom, calls=%fused_computation.243 | custom fusion | bytes 12292 | tf_op jit(solution)/shard_map/scatter | solution.py:105
  329.1 17.4 %gather_fusion.12 = s32[3072]{0:T(1024)S(1)} fusion(s32[3072]{0:T(1024)S(1)} %reshape_squeeze.56, s32[3072]{0:T(1024)S(1)} %fusion.97), kind=kCustom, calls=%fused_computation.8.clone | custom fusion | bytes 36864 | tf_op jit(solution)/shard_map/jit(_take)/gather | solution.py:108
  357.5 55.5 %all-to-all-done.1 = bf16[32,4,96,384]{3,2,1,0:T(8,128)(2,1)} async-done(((bf16[32,4,96,384]{3,2,1,0:T(8,128)(2,1)}), bf16[32,4,96,384]{3,2,1,0:T(8,128)(2,1)}, u32[]{:S(2)}, u32[]{:S(2)}) %all-to-all-start.1) | async-done | bytes 9437216 | tf_op jit(solution)/shard_map/all_to_all | solution.py:153
  413.0 6.5 fusion.114
  419.4 14.7 %gather_fusion.4 = bf16[3072,384]{1,0:T(8,128)(2,1)} fusion(bf16[3072,384]{1,0:T(8,128)(2,1)} %bitcast.130, s32[3072]{0:T(1024)S(1)} %fusion.91), kind=kCustom, calls=%fused_computation.clone | custom fusion | bytes 4730880 | tf_op jit(solution)/shard_map/jit(_take)/gather | solution.py:107
  438.7 24.5 %while.157 = (s32[]{:T(128)}, bf16[3072,128]{1,0:T(8,128)(2,1)S(1)}, s32[]{:T(128)}, s32[6]{0:T(128)}, bf16[3072,128]{1,0:T(8,128)(2,1)}, /*index=5*/s32[3072]{0...) while((s32[]{:T(128)}, bf16[3072,128]{1,0:T(8,128)(2,1)S(1)}, ...), condition=%wide.region_20.23_spmd, body=%wide.region_15.22_spmd.sunk | while | flops 139988512 | bytes 5065506 | solution.py:76
  463.2 16.0 %gather_fusion.7 = bf16[3072,384]{1,0:T(8,128)(2,1)} fusion(bf16[3072,384]{1,0:T(8,128)(2,1)} %bitcast.129, s32[3072]{0:T(1024)} %copy-done.10), kind=kCustom, calls=%fused_computation.3.clone | custom fusion | bytes 4730880 | tf_op jit(solution)/shard_map/jit(_take)/gather | solution.py:107
  483.8 24.8 %while.159 = (s32[]{:T(128)}, bf16[3072,128]{1,0:T(8,128)(2,1)S(1)}, s32[]{:T(128)}, s32[6]{0:T(128)}, bf16[3072,128]{1,0:T(8,128)(2,1)}, /*index=5*/s32[3072]{0...) while((s32[]{:T(128)}, bf16[3072,128]{1,0:T(8,128)(2,1)S(1)}, ...), condition=%wide.region_31.35_spmd, body=%wide.region_26.34_spmd.sunk | while | flops 139988512 | bytes 5065506 | solution.py:76
  508.6 14.0 %gather_fusion.10 = bf16[3072,384]{1,0:T(8,128)(2,1)} fusion(bf16[3072,384]{1,0:T(8,128)(2,1)S(1)} %bitcast.128, s32[3072]{0:T(1024)} %copy-done.9), kind=kCustom, calls=%fused_computation.4.clone | custom fusion | bytes 4730880 | tf_op jit(solution)/shard_map/jit(_take)/gather | solution.py:107
  528.1 24.8 %while.161 = (s32[]{:T(128)}, bf16[3072,128]{1,0:T(8,128)(2,1)}, s32[]{:T(128)}, s32[6]{0:T(128)S(1)}, bf16[3072,128]{1,0:T(8,128)(2,1)}, /*index=5*/s32[3072]{0...) while((s32[]{:T(128)}, bf16[3072,128]{1,0:T(8,128)(2,1)}, ...), condition=%wide.region_42.46_spmd, body=%wide.region_37.45_spmd.sunk | while | flops 139988512 | bytes 5065506 | solution.py:76
  552.9 14.0 %gather_fusion.13 = bf16[3072,384]{1,0:T(8,128)(2,1)} fusion(bf16[3072,384]{1,0:T(8,128)(2,1)S(1)} %bitcast.127, s32[3072]{0:T(1024)} %copy-done.8), kind=kCustom, calls=%fused_computation.5.clone | custom fusion | bytes 4730880 | tf_op jit(solution)/shard_map/jit(_take)/gather | solution.py:107
  571.5 19.5 %while.163 = (s32[]{:T(128)}, bf16[3072,128]{1,0:T(8,128)(2,1)S(1)}, s32[]{:T(128)}, s32[6]{0:T(128)S(1)}, bf16[3072,128]{1,0:T(8,128)(2,1)S(1)}, /*index=5*/s32...) while((s32[]{:T(128)}, bf16[3072,128]{1,0:T(8,128)(2,1)S(1)}, ...), condition=%wide.region_53.57_spmd, body=%wide.region_48.56_spmd.sunk | while | flops 139988512 | bytes 5065506 | solution.py:76
  591.1 10.6 %gather_fusion.5 = bf16[3072,128]{1,0:T(8,128)(2,1)S(1)} fusion(bf16[3072,128]{1,0:T(8,128)(2,1)S(1)} %copy-done.2, s32[3072]{0:T(1024)} %fusion.92), kind=kCustom, calls=%fused_computation.2.clone | custom fusion | bytes 1585152 | tf_op jit(solution)/shard_map/jit(_take)/gather | solution.py:111
  603.3 11.5 %gather_fusion.8 = bf16[3072,128]{1,0:T(8,128)(2,1)} fusion(bf16[3072,128]{1,0:T(8,128)(2,1)S(1)} %get-tuple-element.665, s32[3072]{0:T(1024)S(1)} %copy-done.15), kind=kCustom, calls=%fused_computation.9.clone | custom fusion | bytes 1585152 | tf_op jit(solution)/shard_map/jit(_take)/gather | solution.py:111
  617.6 11.5 %gather_fusion.11 = bf16[3072,128]{1,0:T(8,128)(2,1)} fusion(bf16[3072,128]{1,0:T(8,128)(2,1)S(1)} %copy-done.3, s32[3072]{0:T(1024)S(1)} %copy-done.14), kind=kCustom, calls=%fused_computation.10.clone | custom fusion | bytes 1585152 | tf_op jit(solution)/shard_map/jit(_take)/gather | solution.py:111
  631.7 11.5 %gather_fusion.14 = bf16[3072,128]{1,0:T(8,128)(2,1)} fusion(bf16[3072,128]{1,0:T(8,128)(2,1)S(1)} %get-tuple-element.667, s32[3072]{0:T(1024)S(1)} %copy-done.13), kind=kCustom, calls=%fused_computation.11.clone | custom fusion | bytes 1585152 | tf_op jit(solution)/shard_map/jit(_take)/gather | solution.py:111
  647.7 46.1 %all-to-all-start.2 = ((bf16[32,4,96,128]{3,2,1,0:T(8,128)(2,1)}), bf16[32,4,96,128]{3,2,1,0:T(8,128)(2,1)S(1)}, u32[]{:S(2)}, u32[]{:S(2)}) async-start(bf16[32,4,96,128]{3,2,1,0:T(8,128)(2,1)} %pad_maximum_fusion.1), calls=%async_computation.2 | async-start | bytes 6291456 | tf_op jit(solution)/shard_map/all_to_all | solution.py:156
  694.2 71.0 %all-to-all-done.2 = bf16[32,4,96,128]{3,2,1,0:T(8,128)(2,1)S(1)} async-done(((bf16[32,4,96,128]{3,2,1,0:T(8,128)(2,1)}), bf16[32,4,96,128]{3,2,1,0:T(8,128)(2,1)S(1)}, u32[]{:S(2)}, u32[]{:S(2)}) %all-to-all-start.2) | async-done | bytes 3145760 | tf_op jit(solution)/shard_map/all_to_all | solution.py:156
  765.2 15.0 %gather_fusion.2 = bf16[4096,128]{1,0:T(8,128)(2,1)} fusion(bf16[12288,128]{1,0:T(8,128)(2,1)S(1)} %bitcast.131, s32[4096]{0:T(1024)S(1)} %broadcast_clamp_fusion), kind=kCustom, calls=%fused_computation.14 | custom fusion | bytes 2113536 | tf_op jit(solution)/shard_map/jit(_take)/gather | solution.py:158
  (402 shorter events, 213.1 us)
Async XLA Ops:
  37.5 1.0 copy-start.7
  39.8 15.6 %copy-start.11 = (s32[4096,1]{0,1:T(1,128)}, s32[4096,1]{0,1:T(1,128)S(1)}, u32[]{:S(2)}) copy-start(s32[4096,1]{0,1:T(1,128)S(1)} %compare_select_fusion.10) | copy-start | bytes 49156
  56.0 76.7 %copy-start.4 = (bf16[1024,512]{1,0:T(8,128)(2,1)S(1)}, bf16[1024,512]{1,0:T(8,128)(2,1)}, u32[]{:S(2)}) copy-start(bf16[1024,512]{1,0:T(8,128)(2,1)} %param.26) | copy-start | bytes 3145732
  124.0 10.2 %copy-start.5 = (bf16[1024,512]{1,0:T(8,128)(2,1)S(1)}, bf16[1024,512]{1,0:T(8,128)(2,1)}, u32[]{:S(2)}) copy-start(bf16[1024,512]{1,0:T(8,128)(2,1)} %param.27) | copy-start | bytes 3145732
  124.6 11.0 %copy-start.6 = (bf16[1024,512]{1,0:T(8,128)(2,1)S(1)}, bf16[1024,512]{1,0:T(8,128)(2,1)}, u32[]{:S(2)}) copy-start(bf16[1024,512]{1,0:T(8,128)(2,1)} %param.28) | copy-start | bytes 3145732
  125.4 72.6 %all-to-all-start = ((s32[32,4,96]{2,1,0:T(4,128)}), s32[32,4,96]{2,1,0:T(4,128)S(1)}, u32[]{:S(2)}, u32[]{:S(2)}) async-start(s32[32,4,96]{2,1,0:T(4,128)} %copy.77), calls=%async_computation | async-start | bytes 131072 | tf_op jit(solution)/shard_map/all_to_all | solution.py:154
  198.0 215.0 %all-to-all-start.1 = ((bf16[32,4,96,384]{3,2,1,0:T(8,128)(2,1)}), bf16[32,4,96,384]{3,2,1,0:T(8,128)(2,1)}, u32[]{:S(2)}, u32[]{:S(2)}) async-start(bf16[32,4,96,384]{3,2,1,0:T(8,128)(2,1)} %broadcast_select_fusion), calls=%async_computation.1 | async-start | bytes 18874368 | tf_op jit(solution)/shard_map/all_to_all | solution.py:153
  234.9 17.4 %copy-start.10 = (s32[3072]{0:T(1024)}, s32[3072]{0:T(1024)S(1)}, u32[]{:S(2)}) copy-start(s32[3072]{0:T(1024)S(1)} %fusion.93) | copy-start | bytes 36868
  299.6 17.4 %copy-start.9 = (s32[3072]{0:T(1024)}, s32[3072]{0:T(1024)S(1)}, u32[]{:S(2)}) copy-start(s32[3072]{0:T(1024)S(1)} %fusion.95) | copy-start | bytes 36868
  329.1 17.4 %copy-start.8 = (s32[3072]{0:T(1024)}, s32[3072]{0:T(1024)S(1)}, u32[]{:S(2)}) copy-start(s32[3072]{0:T(1024)S(1)} %fusion.97) | copy-start | bytes 36868
  463.2 16.0 %copy-start.1 = (bf16[3072,128]{1,0:T(8,128)(2,1)}, bf16[3072,128]{1,0:T(8,128)(2,1)S(1)}, u32[]{:S(2)}) copy-start(bf16[3072,128]{1,0:T(8,128)(2,1)S(1)} %get-tuple-element.664) | copy-start | bytes 2359300
  463.2 16.0 %copy-start.18 = (pred[3072]{0:T(1024)(128)(4,1)S(1)}, pred[3072]{0:T(1024)(128)(4,1)}, u32[]{:S(2)}) copy-start(pred[3072]{0:T(1024)(128)(4,1)} %get-tuple-element.947) | copy-start | bytes 9220
  525.5 2.6 copy-start.24
  528.1 24.8 %copy-start = (bf16[32,1,96,384]{3,2,1,0:T(8,128)(2,1)S(1)}, bf16[32,1,96,384]{3,2,1,0:T(8,128)(2,1)}, u32[]{:S(2)}) copy-start(bf16[32,1,96,384]{3,2,1,0:T(8,128)(2,1)} %get-tuple-element.969) | copy-start | bytes 7077892
  552.9 14.0 %copy-start.17 = (pred[3072]{0:T(1024)(128)(4,1)S(1)}, pred[3072]{0:T(1024)(128)(4,1)}, u32[]{:S(2)}) copy-start(pred[3072]{0:T(1024)(128)(4,1)} %get-tuple-element.951) | copy-start | bytes 9220
  569.8 1.7 copy-start.23
  571.5 19.5 %copy-start.2 = (bf16[3072,128]{1,0:T(8,128)(2,1)S(1)}, bf16[3072,128]{1,0:T(8,128)(2,1)}, u32[]{:S(2)}) copy-start(bf16[3072,128]{1,0:T(8,128)(2,1)} %copy-done.1) | copy-start | bytes 2359300
  591.0 10.7 %copy-start.22 = (pred[3072]{0:T(1024)(128)(4,1)S(1)}, pred[3072]{0:T(1024)(128)(4,1)}, u32[]{:S(2)}) copy-start(pred[3072]{0:T(1024)(128)(4,1)} %compare_and_fusion.8) | copy-start | bytes 9220
  591.1 12.3 %copy-start.15 = (s32[3072]{0:T(1024)S(1)}, s32[3072]{0:T(1024)}, u32[]{:S(2)}) copy-start(s32[3072]{0:T(1024)} %fusion.94) | copy-start | bytes 36868
  603.3 11.6 %copy-start.21 = (pred[3072]{0:T(1024)(128)(4,1)S(1)}, pred[3072]{0:T(1024)(128)(4,1)}, u32[]{:S(2)}) copy-start(pred[3072]{0:T(1024)(128)(4,1)} %compare_and_fusion.6) | copy-start | bytes 9220
  603.3 14.2 %copy-start.14 = (s32[3072]{0:T(1024)S(1)}, s32[3072]{0:T(1024)}, u32[]{:S(2)}) copy-start(s32[3072]{0:T(1024)} %fusion.96) | copy-start | bytes 36868
  614.9 2.7 copy-start.3
  617.5 11.6 %copy-start.20 = (pred[3072]{0:T(1024)(128)(4,1)S(1)}, pred[3072]{0:T(1024)(128)(4,1)}, u32[]{:S(2)}) copy-start(pred[3072]{0:T(1024)(128)(4,1)} %compare_and_fusion.4) | copy-start | bytes 9220
  617.6 14.1 %copy-start.13 = (s32[3072]{0:T(1024)S(1)}, s32[3072]{0:T(1024)}, u32[]{:S(2)}) copy-start(s32[3072]{0:T(1024)} %fusion.98) | copy-start | bytes 36868
  631.7 11.6 %copy-start.19 = (pred[3072]{0:T(1024)(128)(4,1)S(1)}, pred[3072]{0:T(1024)(128)(4,1)}, u32[]{:S(2)}) copy-start(pred[3072]{0:T(1024)(128)(4,1)} %compare_and_fusion.2) | copy-start | bytes 9220
  647.7 46.1 %copy-start.16 = (pred[1024,4]{0,1:T(4,128)(4,1)S(1)}, pred[1024,4]{0,1:T(4,128)(4,1)}, u32[]{:S(2)}) copy-start(pred[1024,4]{0,1:T(4,128)(4,1)} %get-tuple-element.942) | copy-start | bytes 12292
  647.7 46.4 %copy-start.12 = (s32[4096,1]{0,1:T(1,128)S(1)}, s32[4096,1]{0,1:T(1,128)}, u32[]{:S(2)}) copy-start(s32[4096,1]{0,1:T(1,128)} %copy-done.11) | copy-start | bytes 49156
  647.7 117.5 %all-to-all-start.2 = ((bf16[32,4,96,128]{3,2,1,0:T(8,128)(2,1)}), bf16[32,4,96,128]{3,2,1,0:T(8,128)(2,1)S(1)}, u32[]{:S(2)}, u32[]{:S(2)}) async-start(bf16[32,4,96,128]{3,2,1,0:T(8,128)(2,1)} %pad_maximum_fusion.1), calls=%async_computation.2 | async-start | bytes 6291456 | tf_op jit(solution)/shard_map/all_to_all | solution.py:156
where the time goes:
time: 796 us; the launch traced here: 787 us
  local copies, waits for them, and re-layouts  436 us (55%)
  waiting for transfers between devices  126 us (16%)
  other arithmetic  115 us (14%)
  starting transfers between devices  59.6 us (7%)
  matrix products  36.3 us (5%)
  loops' own time  9.79 us (1%)
    all_to_all x1, waiting for transfers between devices, local(): lax.all_to_all(answer, ('grp', 'ctx'), split_axis=0, concat_axis=0, tiled...  71 us
    gather x4, local copies, waits for them, and re-layouts, serve_items(): jnp.take(label_data, source_of_row, axis=0, mode='fill', fill_value=-1)  69.6 us
    gather x3, local copies, waits for them, and re-layouts, local(): jnp.take(cluster_ids.T.reshape(-1), source_of_slot, axis=0, mode='fill',...  68.3 us
    gather x4, local copies, waits for them, and re-layouts, serve_items(): jnp.take(row_data, source_of_row, axis=0, mode='fill', fill_value=0)  58.8 us
    all_to_all x1, waiting for transfers between devices, local(): lax.all_to_all(outgoing, ('grp', 'ctx'), split_axis=0, concat_axis=0, til...  55.5 us
    gather x1, local copies, waits for them, and re-layouts, local(): jnp.take(packed_flat, source_of_slot, axis=0, mode='fill', fill_value=0)  49.2 us
    scatter x4, local copies, waits for them, and re-layouts, serve_items(): source_of_row = jnp.full((WORK,), row_total, jnp.int32).at[target_rows].s...  47.4 us
    all_to_all x1, starting transfers between devices, local(): lax.all_to_all(answer, ('grp', 'ctx'), split_axis=0, concat_axis=0, tiled...  46.1 us
  transfers between devices with their start and end apart: 3, of which 2 were waited for; matrix products, arithmetic and copies ran while one was open for 27% of the time, Pallas kernels for 0%

commit v1 on v0

v1 whole, which is shorter than its diff:
```python
import functools
import math

import jax
import jax.numpy as jnp
from jax import lax
from jax.experimental import pallas as pl
from jax.experimental.pallas import tpu as pltpu
from jax.sharding import PartitionSpec as P

CL_SHIFT = 3
LANES = 128
SUB = 16
NEG_FILL = -1e30
F32 = jnp.float32
BF16 = jnp.bfloat16


def up(value, step):
    return (value + step - 1) // step * step


class Plan:
    def __init__(self, devices, heads, tokens):
        self.devices, self.heads, self.tokens = devices, heads, tokens
        self.cap = tokens // devices
        self.busy = 3 * tokens // devices
        self.stride = up(self.cap, SUB)
        self.bstride = up(self.busy, SUB)
        self.servers = devices // heads
        self.share = -(-self.busy // self.servers)
        self.base = devices * self.stride
        self.qstride = up(self.share, SUB)
        self.extra = self.servers * self.qstride
        self.row_k = heads * 3 * self.stride
        self.row_v = self.row_k + self.bstride
        self.row_q = self.row_v + self.bstride
        self.row_l = self.row_q + self.qstride
        self.rows = self.row_l + SUB
        self.ans_q = heads * self.stride
        self.ans_rows = self.ans_q + self.qstride


def iota(shape, dim):
    return lax.broadcasted_iota(jnp.int32, shape, dim)


def dot(a, b):
    return jnp.dot(a, b, preferred_element_type=F32)


def dot_t(a, b):
    return lax.dot_general(a, b, (((1,), (1,)), ((), ())), preferred_element_type=F32)


def onehot(cond):
    return jnp.where(cond, 1.0, 0.0).astype(BF16)


def shift_of(value):
    assert value & (value - 1) == 0
    return value.bit_length() - 1


def pack(p, ids_ref, q_ref, k_ref, v_ref, send_ref, key_ref):
    n, t = p.devices, p.tokens
    earlier = onehot(iota((t, t), 0) < iota((t, t), 1))
    label_sum = jnp.zeros((n, LANES), F32)
    busy_sum = jnp.zeros((n, LANES), F32)
    for h in range(p.heads):
        ids = ids_ref[h : h + 1, :]
        owner = lax.shift_right_logical(ids, CL_SHIFT)
        label = ((ids & (2**CL_SHIFT - 1)) + 1).astype(F32)
        member = jnp.where(iota((n, t), 0) == owner, 1.0, 0.0)
        rank = dot(member.astype(BF16), earlier)
        slot = jnp.sum(member * rank, axis=0, keepdims=True)
        full = jnp.where(jnp.sum(member, axis=1, keepdims=True) > p.cap, 1.0, 0.0)
        is_busy = jnp.sum(member * full, axis=0, keepdims=True) > 0.5
        share_pos = jnp.floor((slot + 0.5) * (1.0 / p.share))
        key_ref[h : h + 1, :] = jnp.where(
            is_busy,
            p.base + slot + share_pos * (p.qstride - p.share),
            owner.astype(F32) * p.stride + slot,
        )
        slot_i = slot.astype(jnp.int32)
        key = jnp.where(is_busy, -1, owner * p.stride + slot_i)
        rank_busy = jnp.where(is_busy, slot_i, -1)
        place = jnp.where(is_busy, -1, h * p.stride + slot_i)
        columns = pl.ds(h * LANES, LANES)
        data = jnp.concatenate([q_ref[:, columns], k_ref[:, columns], v_ref[:, columns]], axis=1)
        select = onehot(iota((p.base, t), 0) == key)
        moved = dot(select, data).astype(BF16)
        for part in range(3):
            row = (3 * h + part) * p.stride
            send_ref[:, row : row + p.stride, :] = moved[
                :, part * LANES : (part + 1) * LANES
            ].reshape(n, p.stride, LANES)
        rows = iota((p.bstride, t), 0)
        moved = dot(onehot(rows == rank_busy), data[:, LANES:]).astype(BF16)
        for j in range(p.servers):
            target = h * p.servers + j
            send_ref[target, p.row_k : p.row_k + p.bstride, :] = moved[:, :LANES]
            send_ref[target, p.row_v : p.row_v + p.bstride, :] = moved[:, LANES:]
        rows = iota((p.extra, t), 0)
        within = rows & (p.qstride - 1)
        wanted = lax.shift_right_logical(rows, shift_of(p.qstride)) * p.share + within
        wanted = jnp.where(within < p.share, wanted, -2)
        moved = dot(onehot(wanted == rank_busy), data[:, :LANES]).astype(BF16)
        first = h * p.servers
        send_ref[first : first + p.servers, p.row_q : p.row_q + p.qstride, :] = moved.reshape(
            p.servers, p.qstride, LANES
        )
        spot = onehot(iota((LANES, t), 0) == place)
        label_sum += dot_t((member * label).astype(BF16), spot)
        spot = onehot(iota((LANES, t), 0) == rank_busy)
        line = dot_t(jnp.broadcast_to(label, (8, t)).astype(BF16), spot)[:1]
        mine = lax.shift_right_logical(iota((n, LANES), 0), shift_of(p.servers)) == h
        busy_sum += jnp.where(mine, jnp.broadcast_to(line, (n, LANES)), 0.0)
    rows, target = iota((n * SUB, n), 0), iota((n * SUB, n), 1)
    same = (rows >> shift_of(SUB)) == target
    lower = (rows & (SUB - 1)) < SUB // 2
    both = dot(onehot(same & lower), label_sum.astype(BF16)) + dot(
        onehot(same & jnp.logical_not(lower)), busy_sum.astype(BF16)
    )
    send_ref[:, p.row_l : p.row_l + SUB, :] = both.astype(BF16).reshape(n, SUB, LANES)


def softmax_rows(scores, allowed, values, factor):
    masked = jnp.where(allowed, scores, NEG_FILL)
    top = jnp.max(masked, axis=1, keepdims=True)
    weights = jnp.exp2((masked - top) * factor)
    total = jnp.sum(weights, axis=1, keepdims=True)
    return (dot(weights.astype(BF16), values) / total).astype(BF16)


def attend(p, me, recv_ref, ans_ref):
    n = p.devices
    factor = LANES**-0.5 * math.log2(math.e)
    label_block = recv_ref[:, p.row_l : p.row_l + SUB, :].reshape(n * SUB, LANES)
    pick = iota((n, n * SUB), 1) - iota((n, n * SUB), 0) * SUB
    labels = dot(onehot(pick == 0), label_block).astype(BF16)
    busy_labels = dot(onehot(pick == SUB // 2), label_block).astype(BF16)

    def lane_labels(table, width, offset):
        total = n * width
        lane = iota((n, total), 1)
        group = jnp.floor((iota((1, total), 1).astype(F32) + 0.5) * (1.0 / width)).astype(
            jnp.int32
        )
        within = iota((1, total), 1) - group * width
        spread = dot(table, onehot(iota((LANES, total), 0) == within + offset))
        return jnp.sum(jnp.where(iota((n, total), 0) == group, spread, 0.0), axis=0, keepdims=True)

    def row_labels(table, width, offset):
        total = n * width
        rows = iota((total, n), 0)
        shift = shift_of(width)
        spread = dot(onehot((rows >> shift) == iota((total, n), 1)), table)
        lane = (iota((total, LANES), 0) & (width - 1)) + offset
        return jnp.sum(
            jnp.where(iota((total, LANES), 1) == lane, spread, 0.0), axis=1, keepdims=True
        )

    block = math.gcd(n, max(1, 256 // p.stride))
    for h in range(p.heads):
        key_label = lane_labels(labels, p.stride, h * p.stride)
        query_label = row_labels(labels, p.stride, h * p.stride)
        row = 3 * h * p.stride
        for start in range(0, n, block):
            size, keys = block * p.stride, (start + block) * p.stride
            first = start * p.stride
            queries = recv_ref[start : start + block, row : row + p.stride, :]
            keys_part = recv_ref[: start + block, row + p.stride : row + 2 * p.stride, :]
            values = recv_ref[: start + block, row + 2 * p.stride : row + 3 * p.stride, :]
            scores = dot_t(queries.reshape(size, LANES), keys_part.reshape(keys, LANES))
            allowed = (query_label[first : first + size] == key_label[:, :keys]) & (
                iota((size, keys), 1) <= iota((size, keys), 0) + first
            )
            out = softmax_rows(scores, allowed, values.reshape(keys, LANES), factor)
            ans_ref[start : start + block, h * p.stride : (h + 1) * p.stride, :] = out.reshape(
                block, p.stride, LANES
            )
    share_first = lax.rem(me, p.servers) * p.share
    key_label = lane_labels(busy_labels, p.bstride, 0)
    query_label = row_labels(busy_labels, p.qstride, share_first)
    block = math.gcd(n, max(1, 128 // p.qstride))
    for start in range(0, n, block):
        size, keys = block * p.qstride, (start + block) * p.bstride
        first = start * p.qstride
        queries = recv_ref[start : start + block, p.row_q : p.row_q + p.qstride, :]
        keys_part = recv_ref[: start + block, p.row_k : p.row_k + p.bstride, :]
        values = recv_ref[: start + block, p.row_v : p.row_v + p.bstride, :]
        scores = dot_t(queries.reshape(size, LANES), keys_part.reshape(keys, LANES))
        rows = iota((size, 1), 0)
        place = (
            ((rows >> shift_of(p.qstride)) + start) * p.bstride
            + (rows & (p.qstride - 1))
            + share_first
        )
        allowed = (query_label[first : first + size] == key_label[:, :keys]) & (
            iota((size, keys), 1) <= place
        )
        out = softmax_rows(scores, allowed, values.reshape(keys, LANES), factor)
        ans_ref[start : start + block, p.ans_q : p.ans_q + p.qstride, :] = out.reshape(
            block, p.qstride, LANES
        )


def unpack(p, key_ref, back_ref, out_ref):
    n, t = p.devices, p.tokens
    keys = jnp.concatenate([key_ref[...]] + [jnp.zeros((8 - p.heads, t), F32)], axis=0)
    key_columns = jnp.transpose(keys).astype(jnp.int32)
    total = p.base + p.extra
    for h in range(p.heads):
        select = onehot(iota((t, total), 1) == key_columns[:, h : h + 1])
        rows = back_ref[:, h * p.stride : (h + 1) * p.stride, :].reshape(p.base, LANES)
        first = h * p.servers
        more = back_ref[first : first + p.servers, p.ans_q : p.ans_q + p.qstride, :]
        rows = jnp.concatenate([rows, more.reshape(p.extra, LANES)], axis=0)
        out_ref[:, h * LANES : (h + 1) * LANES] = dot(select, rows).astype(BF16)


VMEM_SPEC = pl.BlockSpec(memory_space=pltpu.VMEM)
PARAMS = dict(vmem_limit_bytes=56 * 2**20)


def local(query_rows, key_rows, value_rows, cluster_ids):
    axes = ("grp", "ctx")
    devices = lax.axis_size("grp") * lax.axis_size("ctx")
    heads, tokens = cluster_ids.shape
    p = Plan(devices, heads, tokens)

    def pack_kernel(*refs):
        pack(p, *refs)

    def attend_kernel(recv_ref, ans_ref):
        me = lax.axis_index("grp") * lax.axis_size("ctx") + lax.axis_index("ctx")
        attend(p, me, recv_ref, ans_ref)

    def unpack_kernel(*refs):
        unpack(p, *refs)

    send, keys = pl.pallas_call(
        pack_kernel,
        out_shape=(
            jax.ShapeDtypeStruct((devices, p.rows, LANES), BF16),
            jax.ShapeDtypeStruct((heads, tokens), F32),
        ),
        in_specs=[VMEM_SPEC] * 4,
        out_specs=(VMEM_SPEC, VMEM_SPEC),
        compiler_params=pltpu.CompilerParams(**PARAMS),
    )(cluster_ids, query_rows, key_rows, value_rows)
    recv = lax.all_to_all(send, axes, split_axis=0, concat_axis=0, tiled=True)
    ans = pl.pallas_call(
        attend_kernel,
        out_shape=jax.ShapeDtypeStruct((devices, p.ans_rows, LANES), BF16),
        in_specs=[VMEM_SPEC],
        out_specs=VMEM_SPEC,
        compiler_params=pltpu.CompilerParams(**PARAMS),
    )(recv)
    back = lax.all_to_all(ans, axes, split_axis=0, concat_axis=0, tiled=True)
    return pl.pallas_call(
        unpack_kernel,
        out_shape=jax.ShapeDtypeStruct((tokens, heads * LANES), BF16),
        in_specs=[VMEM_SPEC] * 2,
        out_specs=VMEM_SPEC,
        compiler_params=pltpu.CompilerParams(**PARAMS),
    )(keys, back)


def solution(mesh):
    return jax.shard_map(
        local,
        mesh=mesh,
        in_specs=(
            P(("grp", "ctx"), None),
            P(("grp", "ctx"), None),
            P(("grp", "ctx"), None),
            P(None, ("grp", "ctx")),
        ),
        out_specs=P(("grp", "ctx"), None),
        check_vma=False,
    )
```

time: 796 us -> 183 us (0.23); the launches traced: 787 us -> 183 us
  local copies, waits for them, and re-layouts: 436 us -> 0 us
  blocking collectives: 0 us -> 152 us
  waiting for transfers between devices: 126 us -> 0 us
  other arithmetic: 115 us -> 0 us
  starting transfers between devices: 59.6 us -> 0 us
  matrix products: 36.3 us -> 0 us
  Pallas kernels: 0 us -> 30.2 us
  loops' own time: 9.79 us -> 0 us
    gather x18 -> x0, local copies, waits for them, and re-layouts: 308 us -> none  [the longest x4 69.6 us: serve_items(): jnp.take(label_data, source_of_row, axis=0, mode='fill', fill_value=-1)]
    all_to_all x0 -> x2, blocking collectives: none -> 152 us  [the longest x1 118 us: local(): recv = lax.all_to_all(send, axes, split_axis=0, concat_axis=0, tiled=True)]
    all_to_all x3 -> x0, waiting for transfers between devices: 126 us -> none  [the longest x1 71 us: local(): lax.all_to_all(answer, ('grp', 'ctx'), split_axis=0, concat_axis=0, tiled...]
    scatter x5 -> x0, local copies, waits for them, and re-layouts: 62.9 us -> none  [the longest x4 47.4 us: serve_items(): source_of_row = jnp.full((WORK,), row_total, jnp.int32).at[target_rows].s...]
    all_to_all x3 -> x0, starting transfers between devices: 59.6 us -> none  [the longest x1 46.1 us: local(): lax.all_to_all(answer, ('grp', 'ctx'), split_axis=0, concat_axis=0, tiled...]
    another operation x17 -> x0, other arithmetic: 52.1 us -> none
    select_n x39 -> x0, other arithmetic: 38.4 us -> none  [the longest x4 11.5 us: serve_items(): jnp.take(row_data, source_of_row, axis=0, mode='fill', fill_value=0)]
    dynamic_slice x48 -> x0, local copies, waits for them, and re-layouts: 37.7 us -> none  [the longest x12 11.4 us: query_block(): first_block = jnp.minimum(first_live[block_index], row_start) // block_rows]
  transfers between devices with their start and end apart: 3 -> 0, of which waited for: 2 -> 0; matrix products, arithmetic and copies ran while one was open for 27% -> 0% of each run, Pallas kernels for 0% -> 0%
where the time goes in v1:
time: 183 us
  blocking collectives  152 us (83%)
  Pallas kernels  30.2 us (17%)
    all_to_all x1, blocking collectives, local(): recv = lax.all_to_all(send, axes, split_axis=0, concat_axis=0, tiled=True)  118 us
    all_to_all x1, blocking collectives, local(): back = lax.all_to_all(ans, axes, split_axis=0, concat_axis=0, tiled=True)  34.4 us
    pallas_call x1, Pallas kernels, local(): pl.pallas_call(attend_kernel, out_shape=jax.ShapeDtypeStruct((devices, p....  13.5 us
    pallas_call x1, Pallas kernels, local(): pl.pallas_call(pack_kernel, out_shape=(jax.ShapeDtypeStruct((devices, p.r...  11.5 us
    pallas_call x1, Pallas kernels, local(): pl.pallas_call(unpack_kernel, out_shape=jax.ShapeDtypeStruct((tokens, hea...  5.18 us

profile of v1, /device:TPU:0, one launch (start us, length us, event | category | flops | bytes accessed | tf_op | source)
XLA Modules:
  0.0 182.5 jit_solution(15410994441475619449)
XLA Ops:
  0.0 11.5 %shard_map.46 = (bf16[32,608,128]{2,1,0:T(8,128)(2,1)}, f32[4,1024]{1,0:T(4,128)}) custom-call(s32[4,1024]{1,0:T(4,128)} %refs_0_.1, bf16[1024,512]{1,0:T(8,128)(2,1)} %refs_1_.1, bf16[1024,512]{1,0:T(8,128)(2,1)} %refs_2_.1, bf16[1024,512]{1,0:T(8,128)(2,1)} %refs_3_.1), custom_call_target="tpu_custom_call" | custom-call | tf_op jit(solution)/shard_map/pallas_call | solution.py:243
  11.5 117.9 %all_to_all.10.recv_ref = bf16[32,608,128]{2,1,0:T(8,128)(2,1)} all-to-all(bf16[32,608,128]{2,1,0:T(8,128)(2,1)} %get-tuple-element.8), channel_id=1, replica_groups=mesh['grp'=4,'ctx'=8] {'grp','ctx'}, dimensions={0} | all-to-all | bytes 9961472 | tf_op jit(solution)/shard_map/all_to_all | solution.py:253
  129.4 13.5 %shard_map.47 = bf16[32,144,128]{2,1,0:T(8,128)(2,1)} custom-call(bf16[32,608,128]{2,1,0:T(8,128)(2,1)} %all_to_all.10.recv_ref), custom_call_target="tpu_custom_call" | custom-call | tf_op jit(solution)/shard_map/pallas_call | solution.py:254
  142.9 34.4 %all_to_all.11.refs_1_ = bf16[32,144,128]{2,1,0:T(8,128)(2,1)} all-to-all(bf16[32,144,128]{2,1,0:T(8,128)(2,1)} %shard_map.47), channel_id=1, replica_groups=mesh['grp'=4,'ctx'=8] {'grp','ctx'}, dimensions={0} | all-to-all | bytes 2359296 | tf_op jit(solution)/shard_map/all_to_all | solution.py:261
  177.4 5.2 %shard_map.48 = bf16[1024,512]{1,0:T(8,128)(2,1)} custom-call(f32[4,1024]{1,0:T(4,128)} %get-tuple-element.7.refs_0_, bf16[32,144,128]{2,1,0:T(8,128)(2,1)} %all_to_all.11.refs_1_), custom_call_target="tpu_custom_call" | custom-call | tf_op jit(solution)/shard_map/pallas_call | solution.py:262

commit v2 on v1

v2 whole, which is shorter than its diff:
```python
import functools
import math

import jax
import jax.numpy as jnp
from jax import lax
from jax.experimental import pallas as pl
from jax.experimental.pallas import tpu as pltpu
from jax.sharding import PartitionSpec as P

CL_SHIFT = 3
LANES = 128
SUB = 16
NEG_FILL = -1e30
F32 = jnp.float32
BF16 = jnp.bfloat16


def up(value, step):
    return (value + step - 1) // step * step


class Plan:
    def __init__(self, devices, heads, tokens):
        self.devices, self.heads, self.tokens = devices, heads, tokens
        self.cap = tokens // devices
        self.busy = 3 * tokens // devices
        self.stride = up(self.cap, SUB)
        self.per_head = devices // heads
        self.servers = min(self.per_head, max(1, self.busy // 12))
        self.share = -(-self.busy // self.servers)
        self.base = devices * self.stride
        self.qstride = up(self.share, SUB)
        self.extra = self.servers * self.qstride
        self.row_b = heads * 3 * self.stride
        self.row_q = self.row_b + 2 * self.qstride
        self.row_l = self.row_q + self.qstride
        self.rows = self.row_l + SUB
        self.ans_q = heads * self.stride
        self.ans_rows = self.ans_q + self.qstride
        self.chunks = [(self.row_b, self.rows - self.row_b)]
        self.chunks += [(3 * h * self.stride, 3 * self.stride) for h in range(heads)]
        self.ans_chunks = [(self.ans_q, self.qstride)]
        self.ans_chunks += [(h * self.stride, self.stride) for h in range(heads)]


def iota(shape, dim):
    return lax.broadcasted_iota(jnp.int32, shape, dim)


def dot(a, b):
    return jnp.dot(a, b, preferred_element_type=F32)


def dot_t(a, b):
    return lax.dot_general(a, b, (((1,), (1,)), ((), ())), preferred_element_type=F32)


def onehot(cond):
    return jnp.where(cond, 1.0, 0.0).astype(BF16)


def shift_of(value):
    assert value & (value - 1) == 0
    return value.bit_length() - 1


def pack_shared(p, ids_ref, q_ref, k_ref, v_ref, send_ref, key_ref, base_key_ref):
    n, t = p.devices, p.tokens
    earlier = onehot(iota((t, t), 0) < iota((t, t), 1))
    key_ref[...] = jnp.zeros(key_ref.shape, F32)
    label_sum = jnp.zeros((n, LANES), F32)
    busy_sum = jnp.zeros((n, LANES), F32)
    for h in range(p.heads):
        ids = ids_ref[h : h + 1, :]
        owner = lax.shift_right_logical(ids, CL_SHIFT)
        label = ((ids & (2**CL_SHIFT - 1)) + 1).astype(F32)
        member = jnp.where(iota((n, t), 0) == owner, 1.0, 0.0)
        rank = dot(member.astype(BF16), earlier)
        slot = jnp.sum(member * rank, axis=0, keepdims=True)
        full = jnp.where(jnp.sum(member, axis=1, keepdims=True) > p.cap, 1.0, 0.0)
        is_busy = jnp.sum(member * full, axis=0, keepdims=True) > 0.5
        share_pos = jnp.floor((slot + 0.5) * (1.0 / p.share))
        key_ref[h : h + 1, :] = jnp.where(
            is_busy,
            p.base + slot + share_pos * (p.qstride - p.share),
            owner.astype(F32) * p.stride + slot,
        )
        slot_i = slot.astype(jnp.int32)
        base_key_ref[h : h + 1, :] = jnp.where(is_busy, -1, owner * p.stride + slot_i)
        rank_busy = jnp.where(is_busy, slot_i, -1)
        place = jnp.where(is_busy, -1, h * p.stride + slot_i)
        columns = pl.ds(h * LANES, LANES)
        data = jnp.concatenate([k_ref[:, columns], v_ref[:, columns], q_ref[:, columns]], axis=1)
        rows = iota((p.extra, t), 0)
        within = rows & (p.qstride - 1)
        wanted = lax.shift_right_logical(rows, shift_of(p.qstride)) * p.share + within
        wanted = jnp.where(within < p.share, wanted, -2)
        moved = dot(onehot(wanted == rank_busy), data).astype(BF16)
        first = h * p.per_head
        for part in range(3):
            row = p.row_b + part * p.qstride
            send_ref[first : first + p.servers, row : row + p.qstride, :] = moved[
                :, part * LANES : (part + 1) * LANES
            ].reshape(p.servers, p.qstride, LANES)
        if p.servers < p.per_head:
            send_ref[
                first + p.servers : first + p.per_head, p.row_b : p.row_l, :
            ] = jnp.zeros((p.per_head - p.servers, 3 * p.qstride, LANES), BF16)
        spot = onehot(iota((LANES, t), 0) == place)
        label_sum += dot_t((member * label).astype(BF16), spot)
        spot = onehot(iota((LANES, t), 0) == rank_busy)
        line = dot_t(jnp.broadcast_to(label, (8, t)).astype(BF16), spot)[:1]
        mine = lax.shift_right_logical(iota((n, LANES), 0), shift_of(p.per_head)) == h
        busy_sum += jnp.where(mine, jnp.broadcast_to(line, (n, LANES)), 0.0)
    rows, target = iota((n * SUB, n), 0), iota((n * SUB, n), 1)
    same = (rows >> shift_of(SUB)) == target
    lower = (rows & (SUB - 1)) < SUB // 2
    both = dot(onehot(same & lower), label_sum.astype(BF16)) + dot(
        onehot(same & jnp.logical_not(lower)), busy_sum.astype(BF16)
    )
    send_ref[:, p.row_l : p.row_l + SUB, :] = both.astype(BF16).reshape(n, SUB, LANES)


def pack_head(p, h, q_ref, k_ref, v_ref, send_ref, base_key_ref):
    columns = pl.ds(h * LANES, LANES)
    data = jnp.concatenate([q_ref[:, columns], k_ref[:, columns], v_ref[:, columns]], axis=1)
    select = onehot(iota((p.base, p.tokens), 0) == base_key_ref[h : h + 1, :])
    moved = dot(select, data).astype(BF16)
    for part in range(3):
        row = (3 * h + part) * p.stride
        send_ref[:, row : row + p.stride, :] = moved[
            :, part * LANES : (part + 1) * LANES
        ].reshape(p.devices, p.stride, LANES)


def softmax_rows(scores, allowed, values, factor):
    masked = jnp.where(allowed, scores, NEG_FILL)
    top = jnp.max(masked, axis=1, keepdims=True)
    weights = jnp.exp2((masked - top) * factor)
    total = jnp.sum(weights, axis=1, keepdims=True)
    return (dot(weights.astype(BF16), values) / total).astype(BF16)


FACTOR = LANES**-0.5 * math.log2(math.e)


def read_labels(p, recv_ref):
    n = p.devices
    label_block = recv_ref[:, p.row_l : p.row_l + SUB, :].reshape(n * SUB, LANES)
    pick = iota((n, n * SUB), 1) - iota((n, n * SUB), 0) * SUB
    labels = dot(onehot(pick == 0), label_block).astype(BF16)
    busy_labels = dot(onehot(pick == SUB // 2), label_block).astype(BF16)
    return labels, busy_labels


def lane_labels(table, width, lane_of):
    n = table.shape[0]
    total = n * width
    lane = iota((1, total), 1)
    spread = dot(table, onehot(iota((LANES, total), 0) == lane_of(lane & (width - 1))))
    mine = iota((n, total), 0) == (lane >> shift_of(width))
    return jnp.sum(jnp.where(mine, spread, 0.0), axis=0, keepdims=True)


def row_labels(table, width, offset):
    n = table.shape[0]
    total = n * width
    rows = iota((total, n), 0)
    spread = dot(onehot((rows >> shift_of(width)) == iota((total, n), 1)), table)
    lane = (iota((total, LANES), 0) & (width - 1)) + offset
    return jnp.sum(
        jnp.where(iota((total, LANES), 1) == lane, spread, 0.0), axis=1, keepdims=True
    )


def attend_head(p, h, labels, recv_ref, ans_ref):
    n = p.devices
    block = math.gcd(n, max(1, 256 // p.stride))
    key_label = lane_labels(labels, p.stride, lambda within: within + h * p.stride)
    query_label = row_labels(labels, p.stride, h * p.stride)
    row = 3 * h * p.stride
    for start in range(0, n, block):
        size, keys = block * p.stride, (start + block) * p.stride
        first = start * p.stride
        queries = recv_ref[start : start + block, row : row + p.stride, :]
        keys_part = recv_ref[: start + block, row + p.stride : row + 2 * p.stride, :]
        values = recv_ref[: start + block, row + 2 * p.stride : row + 3 * p.stride, :]
        scores = dot_t(queries.reshape(size, LANES), keys_part.reshape(keys, LANES))
        allowed = (query_label[first : first + size] == key_label[:, :keys]) & (
            iota((size, keys), 1) <= iota((size, keys), 0) + first
        )
        out = softmax_rows(scores, allowed, values.reshape(keys, LANES), FACTOR)
        ans_ref[start : start + block, h * p.stride : (h + 1) * p.stride, :] = out.reshape(
            block, p.stride, LANES
        )


def attend_busy(p, me, busy_labels, recv_ref, kv_ref, ans_ref):
    n = p.devices
    mine = lax.rem(me, p.servers)

    def lane_of(within):
        inner = within & (p.qstride - 1)
        return jnp.where(
            inner < p.share, (within >> shift_of(p.qstride)) * p.share + inner, LANES
        )

    key_label = lane_labels(busy_labels, p.extra, lane_of)
    query_label = row_labels(busy_labels, p.qstride, mine * p.share)
    block = math.gcd(n, max(1, 128 // p.qstride))
    for start in range(0, n, block):
        size, keys = block * p.qstride, (start + block) * p.extra
        first = start * p.qstride
        queries = recv_ref[start : start + block, p.row_q : p.row_q + p.qstride, :]
        keys_part = kv_ref[: start + block, :, : p.qstride, :]
        values = kv_ref[: start + block, :, p.qstride :, :]
        scores = dot_t(queries.reshape(size, LANES), keys_part.reshape(keys, LANES))
        rows = iota((size, 1), 0)
        place = (
            ((rows >> shift_of(p.qstride)) + start) * p.extra
            + (rows & (p.qstride - 1))
            + mine * p.qstride
        )
        allowed = (query_label[first : first + size] == key_label[:, :keys]) & (
            iota((size, keys), 1) <= place
        )
        out = softmax_rows(scores, allowed, values.reshape(keys, LANES), FACTOR)
        ans_ref[start : start + block, p.ans_q : p.ans_q + p.qstride, :] = out.reshape(
            block, p.qstride, LANES
        )


def unpack_head(p, h, key_columns, back_ref, out_ref):
    total = p.base + p.extra
    select = onehot(iota((p.tokens, total), 1) == key_columns[:, h : h + 1])
    rows = back_ref[:, h * p.stride : (h + 1) * p.stride, :].reshape(p.base, LANES)
    first = h * p.per_head
    more = back_ref[first : first + p.servers, p.ans_q : p.ans_q + p.qstride, :]
    rows = jnp.concatenate([rows, more.reshape(p.extra, LANES)], axis=0)
    out_ref[:, h * LANES : (h + 1) * LANES] = dot(select, rows).astype(BF16)


def kernel(
    p, groups, members, ids_ref, q_ref, k_ref, v_ref, out_ref,
    send_ref, recv_ref, ans_ref, back_ref, kv_ref, key_ref, base_key_ref,
    send_sem, recv_sem, own_sem,
):
    n = p.devices
    me = lax.axis_index("grp") * members + lax.axis_index("ctx")

    def device(target):
        return (lax.div(target, members), lax.rem(target, members))

    def peer(step):
        hop = lax.rem(step, groups) * members + lax.div(step, groups)
        return lax.rem(me + hop, n)

    barrier = pltpu.get_barrier_semaphore()

    @pl.loop(1, n)
    def _(step):
        pl.semaphore_signal(
            barrier, inc=1, device_id=device(peer(step)), device_id_type=pl.DeviceIdType.MESH
        )

    def start(source, target_ref, row, count, c):
        @pl.loop(1, n)
        def _(step):
            other = peer(step)
            pltpu.make_async_remote_copy(
                src_ref=source.at[other, pl.ds(row, count)],
                dst_ref=target_ref.at[me, pl.ds(row, count)],
                send_sem=send_sem.at[c],
                recv_sem=recv_sem.at[c],
                device_id=device(other),
                device_id_type=pl.DeviceIdType.MESH,
            ).start()

        pltpu.make_async_copy(
            source.at[me, pl.ds(row, count)], target_ref.at[me, pl.ds(row, count)], own_sem.at[c]
        ).start()

    def wait_bytes(ref, row, count, sem):
        part = ref.at[pl.ds(0, n - 1), pl.ds(row, count)]
        pltpu.make_async_copy(part, part, sem).wait()

    def finish(source, target_ref, row, count, c):
        wait_bytes(target_ref, row, count, recv_sem.at[c])
        pltpu.make_async_copy(
            source.at[me, pl.ds(row, count)], target_ref.at[me, pl.ds(row, count)], own_sem.at[c]
        ).wait()

    pack_shared(p, ids_ref, q_ref, k_ref, v_ref, send_ref, key_ref, base_key_ref)
    pl.semaphore_wait(barrier, n - 1)
    start(send_ref, recv_ref, *p.chunks[0], 0)
    for h in range(p.heads):
        pack_head(p, h, q_ref, k_ref, v_ref, send_ref, base_key_ref)
        start(send_ref, recv_ref, *p.chunks[1 + h], 1 + h)

    finish(send_ref, recv_ref, *p.chunks[0], 0)
    mine = lax.rem(me, p.servers)
    shared = recv_ref.at[:, pl.ds(p.row_b, 2 * p.qstride)]
    kv_c = 2 * (p.heads + 1)

    @pl.loop(1, p.servers)
    def _(step):
        other = me - mine + lax.rem(mine + step, p.servers)
        pltpu.make_async_remote_copy(
            src_ref=shared,
            dst_ref=kv_ref.at[:, mine],
            send_sem=send_sem.at[kv_c],
            recv_sem=recv_sem.at[kv_c],
            device_id=device(other),
            device_id_type=pl.DeviceIdType.MESH,
        ).start()

    own = pltpu.make_async_copy(shared, kv_ref.at[:, mine], own_sem.at[kv_c])
    own.start()
    labels, busy_labels = read_labels(p, recv_ref)
    key_columns = jnp.transpose(key_ref[...]).astype(jnp.int32)
    own.wait()
    others = kv_ref.at[:, pl.ds(0, p.servers - 1)]
    pltpu.make_async_copy(others, others, recv_sem.at[kv_c]).wait()
    attend_busy(p, me, busy_labels, recv_ref, kv_ref, ans_ref)
    base_c = p.heads + 1
    start(ans_ref, back_ref, *p.ans_chunks[0], base_c)
    for h in range(p.heads):
        finish(send_ref, recv_ref, *p.chunks[1 + h], 1 + h)
        attend_head(p, h, labels, recv_ref, ans_ref)
        start(ans_ref, back_ref, *p.ans_chunks[1 + h], base_c + 1 + h)
    finish(ans_ref, back_ref, *p.ans_chunks[0], base_c)
    for h in range(p.heads):
        finish(ans_ref, back_ref, *p.ans_chunks[1 + h], base_c + 1 + h)
        unpack_head(p, h, key_columns, back_ref, out_ref)
    for c in range(p.heads + 1):
        wait_bytes(send_ref, *p.chunks[c], send_sem.at[c])
        wait_bytes(ans_ref, *p.ans_chunks[c], send_sem.at[base_c + c])
    pltpu.make_async_copy(others, others, send_sem.at[kv_c]).wait()


VMEM_SPEC = pl.BlockSpec(memory_space=pltpu.VMEM)


def local(query_rows, key_rows, value_rows, cluster_ids):
    groups, members = lax.axis_size("grp"), lax.axis_size("ctx")
    heads, tokens = cluster_ids.shape
    p = Plan(groups * members, heads, tokens)
    count = 2 * (heads + 1) + 1
    return pl.pallas_call(
        functools.partial(kernel, p, groups, members),
        out_shape=jax.ShapeDtypeStruct((tokens, heads * LANES), BF16),
        in_specs=[VMEM_SPEC] * 4,
        out_specs=VMEM_SPEC,
        scratch_shapes=[
            pltpu.VMEM((p.devices, p.rows, LANES), BF16),
            pltpu.VMEM((p.devices, p.rows, LANES), BF16),
            pltpu.VMEM((p.devices, p.ans_rows, LANES), BF16),
            pltpu.VMEM((p.devices, p.ans_rows, LANES), BF16),
            pltpu.VMEM((p.devices, p.servers, 2 * p.qstride, LANES), BF16),
            pltpu.VMEM((up(heads, 8), tokens), F32),
            pltpu.VMEM((up(heads, 8), tokens), jnp.int32),
            pltpu.SemaphoreType.DMA((count,)),
            pltpu.SemaphoreType.DMA((count,)),
            pltpu.SemaphoreType.DMA((count,)),
        ],
        compiler_params=pltpu.CompilerParams(
            collective_id=0, has_side_effects=True, vmem_limit_bytes=60 * 2**20
        ),
    )(cluster_ids, query_rows, key_rows, value_rows)


def solution(mesh):
    return jax.shard_map(
        local,
        mesh=mesh,
        in_specs=(
            P(("grp", "ctx"), None),
            P(("grp", "ctx"), None),
            P(("grp", "ctx"), None),
            P(None, ("grp", "ctx")),
        ),
        out_specs=P(("grp", "ctx"), None),
        check_vma=False,
    )
```

time: 183 us -> 119 us (0.65)
  blocking collectives: 152 us -> 0 us
  Pallas kernels: 30.2 us -> 117 us
  local copies, waits for them, and re-layouts: 0 us -> 2.26 us
    all_to_all x2 -> x0, blocking collectives: 152 us -> none  [the longest x1 118 us: local(): recv = lax.all_to_all(send, axes, split_axis=0, concat_axis=0, tiled=True)]
    pallas_call x3 -> x1, Pallas kernels: 30.2 us -> 117 us  [local(): pl.pallas_call(functools.partial(kernel, p, groups, members), out_shape=j...]
    unnamed x0 -> x1, local copies, waits for them, and re-layouts: none -> 2.26 us
where the time goes in v2:
time: 119 us
  Pallas kernels  117 us (98%)
  local copies, waits for them, and re-layouts  2.26 us (2%)
    pallas_call x1, Pallas kernels, local(): pl.pallas_call(functools.partial(kernel, p, groups, members), out_shape=j...  117 us

profile of v2, /device:TPU:0, one launch (start us, length us, event | category | flops | bytes accessed | tf_op | source)
XLA Modules:
  0.0 119.1 jit_solution(1088693187901890466)
XLA Ops:
  0.0 116.9 %shard_map.46 = bf16[1024,512]{1,0:T(8,128)(2,1)} custom-call(s32[4,1024]{1,0:T(4,128)} %ids_ref.1, bf16[1024,512]{1,0:T(8,128)(2,1)} %q_ref.1, bf16[1024,512]{1,0:T(8,128)(2,1)} %k_ref.1, bf16[1024,512]{1,0:T(8,128)(2,1)} %v_ref.1), custom_call_target="tpu_custom_call" | custom-call | tf_op jit(solution)/shard_map/pallas_call | solution.py:350
  116.9 2.3 %copy.6 = bf16[1024,512]{1,0:T(8,128)(2,1)} copy(bf16[1024,512]{1,0:T(8,128)(2,1)} %shard_map.46) | data formatting | bytes 2097152

commit v3 on v2

--- a/solution.py
+++ b/solution.py
@@ -30,12 +30,11 @@
         self.servers = min(self.per_head, max(1, self.busy // 12))
         self.share = -(-self.busy // self.servers)
         self.base = devices * self.stride
-        self.qstride = up(self.share, SUB)
+        self.qstride = up(self.share + 2, SUB)
         self.extra = self.servers * self.qstride
         self.row_b = heads * 3 * self.stride
         self.row_q = self.row_b + 2 * self.qstride
-        self.row_l = self.row_q + self.qstride
-        self.rows = self.row_l + SUB
+        self.rows = self.row_q + self.qstride
         self.ans_q = heads * self.stride
         self.ans_rows = self.ans_q + self.qstride
         self.chunks = [(self.row_b, self.rows - self.row_b)]
@@ -65,12 +64,13 @@
     return value.bit_length() - 1
 
 
-def pack_shared(p, ids_ref, q_ref, k_ref, v_ref, send_ref, key_ref, base_key_ref):
+def pack_shared(p, ids_ref, q_ref, k_ref, v_ref, send_ref, key_ref, base_key_ref, after_first):
     n, t = p.devices, p.tokens
     earlier = onehot(iota((t, t), 0) < iota((t, t), 1))
     key_ref[...] = jnp.zeros(key_ref.shape, F32)
     label_sum = jnp.zeros((n, LANES), F32)
     busy_sum = jnp.zeros((n, LANES), F32)
+    query_blocks = []
     for h in range(p.heads):
         ids = ids_ref[h : h + 1, :]
         owner = lax.shift_right_logical(ids, CL_SHIFT)
@@ -88,6 +88,8 @@
         )
         slot_i = slot.astype(jnp.int32)
         base_key_ref[h : h + 1, :] = jnp.where(is_busy, -1, owner * p.stride + slot_i)
+        if h == 0:
+            after_first()
         rank_busy = jnp.where(is_busy, slot_i, -1)
         place = jnp.where(is_busy, -1, h * p.stride + slot_i)
         columns = pl.ds(h * LANES, LANES)
@@ -96,30 +98,35 @@
         within = rows & (p.qstride - 1)
         wanted = lax.shift_right_logical(rows, shift_of(p.qstride)) * p.share + within
         wanted = jnp.where(within < p.share, wanted, -2)
-        moved = dot(onehot(wanted == rank_busy), data).astype(BF16)
+        exact = dot(onehot(wanted == rank_busy), data)
+        moved = exact.astype(BF16)
         first = h * p.per_head
-        for part in range(3):
+        for part in range(2):
             row = p.row_b + part * p.qstride
             send_ref[first : first + p.servers, row : row + p.qstride, :] = moved[
                 :, part * LANES : (part + 1) * LANES
             ].reshape(p.servers, p.qstride, LANES)
-        if p.servers < p.per_head:
+        query_blocks.append(exact[:, 2 * LANES :])
+        spare = p.per_head - p.servers
+        if spare > 0:
             send_ref[
-                first + p.servers : first + p.per_head, p.row_b : p.row_l, :
-            ] = jnp.zeros((p.per_head - p.servers, 3 * p.qstride, LANES), BF16)
+                first + p.servers : first + p.per_head, p.row_b : p.row_q, :
+            ] = jnp.zeros((spare, 2 * p.qstride, LANES), BF16)
+            query_blocks.append(jnp.zeros((spare * p.qstride, LANES), F32))
         spot = onehot(iota((LANES, t), 0) == place)
         label_sum += dot_t((member * label).astype(BF16), spot)
         spot = onehot(iota((LANES, t), 0) == rank_busy)
         line = dot_t(jnp.broadcast_to(label, (8, t)).astype(BF16), spot)[:1]
         mine = lax.shift_right_logical(iota((n, LANES), 0), shift_of(p.per_head)) == h
         busy_sum += jnp.where(mine, jnp.broadcast_to(line, (n, LANES)), 0.0)
-    rows, target = iota((n * SUB, n), 0), iota((n * SUB, n), 1)
-    same = (rows >> shift_of(SUB)) == target
-    lower = (rows & (SUB - 1)) < SUB // 2
-    both = dot(onehot(same & lower), label_sum.astype(BF16)) + dot(
-        onehot(same & jnp.logical_not(lower)), busy_sum.astype(BF16)
+    place = iota((n * p.qstride, n), 0) - iota((n * p.qstride, n), 1) * p.qstride
+    both = dot(onehot(place == p.share), label_sum.astype(BF16)) + dot(
+        onehot(place == p.share + 1), busy_sum.astype(BF16)
     )
-    send_ref[:, p.row_l : p.row_l + SUB, :] = both.astype(BF16).reshape(n, SUB, LANES)
+    both += jnp.concatenate(query_blocks, axis=0)
+    send_ref[:, p.row_q : p.row_q + p.qstride, :] = both.astype(BF16).reshape(
+        n, p.qstride, LANES
+    )
 
 
 def pack_head(p, h, q_ref, k_ref, v_ref, send_ref, base_key_ref):
@@ -147,10 +154,11 @@
 
 def read_labels(p, recv_ref):
     n = p.devices
-    label_block = recv_ref[:, p.row_l : p.row_l + SUB, :].reshape(n * SUB, LANES)
-    pick = iota((n, n * SUB), 1) - iota((n, n * SUB), 0) * SUB
-    labels = dot(onehot(pick == 0), label_block).astype(BF16)
-    busy_labels = dot(onehot(pick == SUB // 2), label_block).astype(BF16)
+    total = n * p.qstride
+    label_block = recv_ref[:, p.row_q : p.row_q + p.qstride, :].reshape(total, LANES)
+    pick = iota((n, total), 1) - iota((n, total), 0) * p.qstride
+    labels = dot(onehot(pick == p.share), label_block).astype(BF16)
+    busy_labels = dot(onehot(pick == p.share + 1), label_block).astype(BF16)
     return labels, busy_labels
 
 
@@ -291,10 +299,16 @@
             source.at[me, pl.ds(row, count)], target_ref.at[me, pl.ds(row, count)], own_sem.at[c]
         ).wait()
 
-    pack_shared(p, ids_ref, q_ref, k_ref, v_ref, send_ref, key_ref, base_key_ref)
-    pl.semaphore_wait(barrier, n - 1)
+    def after_first():
+        pack_head(p, 0, q_ref, k_ref, v_ref, send_ref, base_key_ref)
+        pl.semaphore_wait(barrier, n - 1)
+        start(send_ref, recv_ref, *p.chunks[1], 1)
+
+    pack_shared(
+        p, ids_ref, q_ref, k_ref, v_ref, send_ref, key_ref, base_key_ref, after_first
+    )
     start(send_ref, recv_ref, *p.chunks[0], 0)
-    for h in range(p.heads):
+    for h in range(1, p.heads):
         pack_head(p, h, q_ref, k_ref, v_ref, send_ref, base_key_ref)
         start(send_ref, recv_ref, *p.chunks[1 + h], 1 + h)
 
@@ -319,13 +333,14 @@
     own.start()
     labels, busy_labels = read_labels(p, recv_ref)
     key_columns = jnp.transpose(key_ref[...]).astype(jnp.int32)
-    own.wait()
     others = kv_ref.at[:, pl.ds(0, p.servers - 1)]
-    pltpu.make_async_copy(others, others, recv_sem.at[kv_c]).wait()
-    attend_busy(p, me, busy_labels, recv_ref, kv_ref, ans_ref)
     base_c = p.heads + 1
-    start(ans_ref, back_ref, *p.ans_chunks[0], base_c)
     for h in range(p.heads):
+        if h == p.heads - 1:
+            own.wait()
+            pltpu.make_async_copy(others, others, recv_sem.at[kv_c]).wait()
+            attend_busy(p, me, busy_labels, recv_ref, kv_ref, ans_ref)
+            start(ans_ref, back_ref, *p.ans_chunks[0], base_c)
         finish(send_ref, recv_ref, *p.chunks[1 + h], 1 + h)
         attend_head(p, h, labels, recv_ref, ans_ref)
         start(ans_ref, back_ref, *p.ans_chunks[1 + h], base_c + 1 + h)

time: 119 us -> 118 us (level)
  Pallas kernels: 117 us -> 115 us
    pallas_call x1, Pallas kernels: 117 us -> 115 us  [local(): pl.pallas_call(functools.partial(kernel, p, groups, members), out_shape=j...]
where the time goes in v3:
time: 118 us; the launch traced here: 117 us
  Pallas kernels  115 us (97%)
  local copies, waits for them, and re-layouts  2.26 us (2%)
    pallas_call x1, Pallas kernels, local(): pl.pallas_call(functools.partial(kernel, p, groups, members), out_shape=j...  115 us

profile of v3, /device:TPU:0, one launch (start us, length us, event | category | flops | bytes accessed | tf_op | source)
XLA Modules:
  0.0 117.5 jit_solution(2262941409683066769)
XLA Ops:
  0.0 115.2 %shard_map.46 = bf16[1024,512]{1,0:T(8,128)(2,1)} custom-call(s32[4,1024]{1,0:T(4,128)} %ids_ref.1, bf16[1024,512]{1,0:T(8,128)(2,1)} %q_ref.1, bf16[1024,512]{1,0:T(8,128)(2,1)} %k_ref.1, bf16[1024,512]{1,0:T(8,128)(2,1)} %v_ref.1), custom_call_target="tpu_custom_call" | custom-call | tf_op jit(solution)/shard_map/pallas_call | solution.py:365
  115.2 2.3 %copy.6 = bf16[1024,512]{1,0:T(8,128)(2,1)} copy(bf16[1024,512]{1,0:T(8,128)(2,1)} %shard_map.46) | data formatting | bytes 2097152
